TPU v7x, 32 devices: a whole 2x2x4 slice. The times are simulated.
32 devices in a mesh: win: 2 (over y), row: 16 (over z, x, core).
Axes of the slice: x: 2, y: 2, z: 4, core: 2. Of those that a mesh axis runs over, the one named last changes fastest.
Arguments:
- raw: bfloat16 [4096, 16384], P(None, ('win', 'row')), parts along dimension 1, may hold values from -30 to 30, as said below
- fir_taps: float32 [16], replicated, may hold values from -1.5 to 1.5
- band_width: int32 [16], P('row'), may hold values from 1 to 8, as said below
- dead_count: int32 [16], P('row'), may hold values from 0 to 64, as said below
Outputs:
- correlations: bfloat16 [8192, 8, 8, 256], P(('win', 'row')), parts along dimension 0
There are 2 independent parts, one for each index of `win`. A program takes and returns all parts, laid end to end along the dimension named above; an argument that names none is the same for every part. Nothing has to cross between parts.
Inputs may be any that keep to these rules, and one draw needn't show every extreme that they name: `raw`: samples of the record. Row tile t pairs with column tiles t to t + band_width[t] - 1; band_width[t] <= 16 - t, and tile 0 pairs with 8 tiles. `dead_count`: some tile has 64 dead channels.
All inputs are finite; a program needn't handle non-finite values.
Results may differ from a plain program's by a relative error of at most 0.0069.
Values may be sent and summed in bfloat16 or wider, within the bound.
No kernel may reach another device: no remote copies, remote signals or barrier semaphores. Data moves between devices by JAX's collectives and lax.ppermute only.
A program may use at most 128 MiB of HBM per device.

v0:
```python
import math
import jax
import jax.numpy as jnp
from jax import lax
from jax.sharding import PartitionSpec as P

NT = 2048
NF = 512
DEC = 4
TAPS = 16
SMOOTH = 64
LAGS = 8
NB = 8


def from_behind(value, axis, steps):
    count = lax.axis_size(axis)
    initial, last = (max(0, -steps), min(count, count - steps))
    return lax.ppermute(value, axis, [(source, source + steps) for source in range(initial, last)])


def fir_decimate(padded, fir_taps, count):
    left_reach = (TAPS - DEC) // 2
    rows = padded.shape[0]
    width = padded.shape[1]
    phased = jnp.transpose(padded.reshape(rows, width // DEC, DEC), (2, 0, 1))
    filtered = jnp.zeros((rows, count), jnp.float32)
    for tap_index in range(TAPS):
        first_at = 2 * DEC - left_reach + tap_index
        phase_index = first_at % DEC
        block_start = first_at // DEC
        sampled = phased[phase_index, :, block_start : block_start + count]
        filtered = filtered + fir_taps[tap_index] * sampled
    return filtered


def spectral_table():
    sample_ids = jnp.arange(NT, dtype=jnp.int32)[:, None]
    bin_ids = jnp.arange(NF, dtype=jnp.int32)[None, :] + 1
    phases = (sample_ids * bin_ids % NT).astype(jnp.float32) * (2.0 * math.pi / NT)
    return jnp.concatenate([jnp.cos(phases), -jnp.sin(phases)], axis=1).astype(jnp.bfloat16)


def whiten(decimated):
    spectrum = jnp.dot(decimated, spectral_table(), preferred_element_type=jnp.float32)
    real_part = spectrum[:, :NF]
    imag_part = spectrum[:, NF:]
    power_bins = real_part * real_part + imag_part * imag_part
    bin_ids = jnp.arange(NF, dtype=jnp.int32)
    window = (jnp.abs(bin_ids[:, None] - bin_ids[None, :]) <= SMOOTH).astype(jnp.float32)
    counts = jnp.sum(window, axis=0)
    smoothed = (
        jnp.dot(
            power_bins, window, precision=lax.Precision.HIGHEST, preferred_element_type=jnp.float32
        )
        / counts
    )
    factor = lax.rsqrt(smoothed + 1e-05)
    return (real_part * factor, imag_part * factor)


def lag_rows(white_real, white_imag):
    lag_ids = jnp.arange(LAGS, dtype=jnp.int32) - LAGS // 2
    bin_ids = jnp.arange(NF, dtype=jnp.int32) + 1
    phases = ((lag_ids % NT)[:, None] * bin_ids[None, :] % NT).astype(jnp.float32) * (
        2.0 * math.pi / NT
    )
    cosine_table = jnp.cos(phases)[None]
    sine_table = jnp.sin(phases)[None]
    rotated_real = white_real[:, None, :] * cosine_table - white_imag[:, None, :] * sine_table
    rotated_imag = white_real[:, None, :] * sine_table + white_imag[:, None, :] * cosine_table
    stacked = jnp.concatenate([rotated_real, rotated_imag], axis=2).astype(jnp.bfloat16)
    return stacked.reshape(-1, 2 * NF)


def shards(raw, fir_taps, band_width, dead_count):
    band_span = band_width[0]
    dead_here = dead_count[0]
    channel_block = lax.all_to_all(raw, "row", split_axis=0, concat_axis=1, tiled=True)
    padded = jnp.pad(channel_block.astype(jnp.float32), ((0, 0), (2 * DEC, 2 * DEC)))
    filtered = fir_decimate(padded, fir_taps, NT)
    tile_rows = filtered.shape[0]
    keep_mask = (jnp.arange(tile_rows, dtype=jnp.int32) >= dead_here).astype(jnp.float32)[:, None]
    decimated = (filtered * keep_mask).astype(jnp.bfloat16)
    white_real, white_imag = whiten(decimated)
    white = jnp.concatenate([white_real, white_imag], axis=1).astype(jnp.bfloat16)
    lagged = lag_rows(white_real, white_imag)
    column_list = [white]
    for offset in range(1, NB):
        column_list.append(from_behind(white, "row", -offset))
    window_tiles = jnp.stack(column_list, axis=0)
    scales = (jnp.arange(NB, dtype=jnp.int32) < band_span).astype(jnp.float32) / math.sqrt(NF)
    column_block = window_tiles.reshape(NB * tile_rows, 2 * NF)
    product = lax.dot_general(
        lagged, column_block, (((1,), (1,)), ((), ())), preferred_element_type=jnp.float32
    )
    shaped = product.reshape(tile_rows, LAGS, NB, tile_rows)
    return (shaped * scales[None, None, :, None]).astype(jnp.bfloat16)


def solution(mesh):
    return jax.shard_map(
        shards,
        mesh=mesh,
        in_specs=(P(None, ("win", "row")), P(), P("row"), P("row")),
        out_specs=P(("win", "row"), None, None, None),
        check_vma=False,
    )
```

profile of v0, /device:TPU:1, one launch (start us, length us, event | category | flops | bytes accessed | tf_op | source)
XLA Modules:
  0.0 294.4 jit_solution(10741575521673612)
XLA Ops:
  0.0 0.0 copy-start
  0.0 7.5 %all-to-all-start = ((bf16[16,256,512]{2,1,0:T(8,128)(2,1)}), bf16[16,256,512]{2,1,0:T(8,128)(2,1)}, u32[]{:S(2)}, u32[]{:S(2)}) async-start(bf16[16,256,512]{2,1,0:T(8,128)(2,1)} %bitcast.59), calls=%async_computation | async-start | bytes 8388608 | tf_op jit(solution)/shard_map/all_to_all | solution.py:79
  8.8 0.1 convert_reduce_fusion
  8.9 0.0 copy-done
  8.9 0.7 fusion.51
  9.6 0.2 fusion.44
  9.8 18.2 %cosine_convert_fusion = (bf16[2048,512]{1,0:T(8,128)(2,1)S(1)}, bf16[2048,512]{1,0:T(8,128)(2,1)}) fusion(s32[512]{0:T(512)S(1)} %iota_add_fusion), kind=kLoop, calls=%fused_computation.19 | loop fusion | flops 17825792 | bytes 4196352 | tf_op jit(solution)/shard_map/convert.14
  28.0 57.6 %all-to-all-done = bf16[16,256,512]{2,1,0:T(8,128)(2,1)} async-done(((bf16[16,256,512]{2,1,0:T(8,128)(2,1)}), bf16[16,256,512]{2,1,0:T(8,128)(2,1)}, u32[]{:S(2)}, u32[]{:S(2)}) %all-to-all-start) | async-done | bytes 4194336 | tf_op jit(solution)/shard_map/all_to_all | solution.py:79
  85.5 6.4 %copy.11 = bf16[256,16,512]{0,2,1:T(8,128)(2,1)} copy(bf16[256,16,512]{2,0,1:T(8,128)(2,1)} %bitcast.2) | data formatting | bytes 8388608 | tf_op jit(solution)/shard_map/convert_element_type | solution.py:80
  91.9 5.2 %pad_convert_fusion = f32[256,8208]{0,1:T(8,128)} fusion(bf16[256,8192]{0,1:T(8,128)(2,1)} %bitcast.57), kind=kLoop, calls=%fused_computation.4 | loop fusion | flops 2101248 | bytes 12599296 | tf_op jit(solution)/shard_map/transpose | solution.py:26
  97.1 10.1 %reshape.192 = f32[256,2052,4]{0,2,1:T(4,128)} reshape(f32[256,8208]{0,1:T(8,128)} %pad_convert_fusion) | data formatting | bytes 16809984 | tf_op jit(solution)/shard_map/transpose | solution.py:26
  107.2 10.9 %copy.12 = f32[256,2052,4]{1,0,2:T(8,128)} copy(f32[256,2052,4]{0,2,1:T(4,128)} %reshape.192) | data formatting | bytes 16809984 | tf_op jit(solution)/shard_map/transpose | solution.py:26
  118.2 30.3 %fusion.3 = f32[256,1024]{1,0:T(8,128)S(1)} fusion(bf16[2048,512]{1,0:T(8,128)(2,1)} %get-tuple-element.16, bf16[2048,512]{1,0:T(8,128)(2,1)S(1)} %get-tuple-element.15, f32[4,256,2052]{2,1,0:T(8,128)} %bitcast.58, f32[256]{0:T(256)S(1)} %compare_convert_fusion, f32[]{:T(128)} %bitcast.19, f32[]{:T(128)} %bitcast.18, f32[]{:T(128)} %bitcast.17, ...), kind=kOutput, calls=%fused_computation.8 | convolution fusion | flops 1099431936 | bytes 38806528 | tf_op jit(solution)/shard_map/dot_general | solution.py:45
  148.4 0.7 fusion.49
  149.2 0.1 pad_maximum_fusion
  149.2 1.9 collective-permute-start
  151.2 1.3 collective-permute-start.1
  152.5 1.3 collective-permute-start.2
  153.8 1.3 collective-permute-start.3
  155.1 1.3 collective-permute-start.4
  156.4 1.1 subtract_convert_fusion
  157.5 0.1 maximum_dynamic-update-slice_fusion
  157.6 9.5 %collective-permute-done = bf16[256,1024]{1,0:T(8,128)(2,1)S(1)} collective-permute-done((bf16[256,1024]{1,0:T(8,128)(2,1)S(1)}, bf16[256,1024]{1,0:T(8,128)(2,1)S(1)}, u32[]{:S(2)}, u32[]{:S(2)}) %collective-permute-start) | collective-permute-done | bytes 524320 | tf_op jit(solution)/shard_map/ppermute | solution.py:19
  167.0 1.3 collective-permute-start.5
  168.4 3.1 %collective-permute-done.1 = bf16[256,1024]{1,0:T(8,128)(2,1)S(1)} collective-permute-done((bf16[256,1024]{1,0:T(8,128)(2,1)S(1)}, bf16[256,1024]{1,0:T(8,128)(2,1)S(1)}, u32[]{:S(2)}, u32[]{:S(2)}) %collective-permute-start.1) | collective-permute-done | bytes 524320 | tf_op jit(solution)/shard_map/ppermute | solution.py:19
  171.5 1.5 collective-permute-start.6
  173.0 25.6 %collective-permute-done.2 = bf16[256,1024]{1,0:T(8,128)(2,1)S(1)} collective-permute-done((bf16[256,1024]{1,0:T(8,128)(2,1)S(1)}, bf16[256,1024]{1,0:T(8,128)(2,1)S(1)}, u32[]{:S(2)}, u32[]{:S(2)}) %collective-permute-start.2) | collective-permute-done | bytes 524320 | tf_op jit(solution)/shard_map/ppermute | solution.py:19
  198.7 3.9 %collective-permute-done.3 = bf16[256,1024]{1,0:T(8,128)(2,1)S(1)} collective-permute-done((bf16[256,1024]{1,0:T(8,128)(2,1)S(1)}, bf16[256,1024]{1,0:T(8,128)(2,1)S(1)}, u32[]{:S(2)}, u32[]{:S(2)}) %collective-permute-start.3) | collective-permute-done | bytes 524320 | tf_op jit(solution)/shard_map/ppermute | solution.py:19
  202.6 2.3 collective-permute-done.4
  204.9 3.9 %collective-permute-done.5 = bf16[256,1024]{1,0:T(8,128)(2,1)S(1)} collective-permute-done((bf16[256,1024]{1,0:T(8,128)(2,1)S(1)}, bf16[256,1024]{1,0:T(8,128)(2,1)S(1)}, u32[]{:S(2)}, u32[]{:S(2)}) %collective-permute-start.5) | collective-permute-done | bytes 524320 | tf_op jit(solution)/shard_map/ppermute | solution.py:19
  208.8 62.8 %collective-permute-done.6 = bf16[256,1024]{1,0:T(8,128)(2,1)S(1)} collective-permute-done((bf16[256,1024]{1,0:T(8,128)(2,1)S(1)}, bf16[256,1024]{1,0:T(8,128)(2,1)S(1)}, u32[]{:S(2)}, u32[]{:S(2)}) %collective-permute-start.6) | collective-permute-done | bytes 524320 | tf_op jit(solution)/shard_map/ppermute | solution.py:19
  271.6 11.2 %multiply_convert_fusion = bf16[256,8,8,256]{3,0,2,1:T(8,128)(2,1)} fusion(f32[8]{0:T(128)S(1)} %compare_select_fusion.2, bf16[256,8,512]{2,0,1:T(8,128)(2,1)S(1)} %get-tuple-element.12, bf16[256,8,512]{2,0,1:T(8,128)(2,1)S(1)} %get-tuple-element.11, bf16[8,256,1024]{2,1,0:T(8,128)(2,1)S(1)} %bitcast_dynamic-update-slice_fusion), kind=kOutput, calls=%fused_computation | convolution fusion | flops 8606711808 | bytes 16777248 | tf_op jit(solution)/shard_map/dot_general | solution.py:94
  282.8 11.5 %copy.13 = bf16[256,8,8,256]{3,2,1,0:T(8,128)(2,1)} copy(bf16[256,8,8,256]{3,0,2,1:T(8,128)(2,1)} %multiply_convert_fusion) | data formatting | bytes 16777216 | tf_op jit(solution)/shard_map/convert_element_type | solution.py:98
  (11 shorter events, 0.3 us)
Async XLA Ops:
  0.0 8.9 %copy-start = (f32[16]{0:T(128)S(1)}, f32[16]{0:T(128)}, u32[]{:S(2)}) copy-start(f32[16]{0:T(128)} %param.5) | copy-start | bytes 196
  0.0 85.5 %all-to-all-start = ((bf16[16,256,512]{2,1,0:T(8,128)(2,1)}), bf16[16,256,512]{2,1,0:T(8,128)(2,1)}, u32[]{:S(2)}, u32[]{:S(2)}) async-start(bf16[16,256,512]{2,1,0:T(8,128)(2,1)} %bitcast.59), calls=%async_computation | async-start | bytes 8388608 | tf_op jit(solution)/shard_map/all_to_all | solution.py:79
  149.2 17.8 %collective-permute-start = (bf16[256,1024]{1,0:T(8,128)(2,1)S(1)}, bf16[256,1024]{1,0:T(8,128)(2,1)S(1)}, u32[]{:S(2)}, u32[]{:S(2)}) collective-permute-start(bf16[256,1024]{1,0:T(8,128)(2,1)S(1)} %pad_maximum_fusion), channel_id=1, source_target_pairs={{1,0},{2,1},{3,2},{4,3},{5,4},{6,5},{7,6},{8,7},{9,8},{10,9},{11,1... | collective-permute-start | bytes 1572872 | tf_op jit(solution)/shard_map/ppermute | solution.py:19
  151.2 20.3 %collective-permute-start.1 = (bf16[256,1024]{1,0:T(8,128)(2,1)S(1)}, bf16[256,1024]{1,0:T(8,128)(2,1)S(1)}, u32[]{:S(2)}, u32[]{:S(2)}) collective-permute-start(bf16[256,1024]{1,0:T(8,128)(2,1)S(1)} %pad_maximum_fusion), channel_id=1, source_target_pairs={{2,0},{3,1},{4,2},{5,3},{6,4},{7,5},{8,6},{9,7},{10,8},{11,9},{12,... | collective-permute-start | bytes 1572872 | tf_op jit(solution)/shard_map/ppermute | solution.py:19
  152.5 46.2 %collective-permute-start.2 = (bf16[256,1024]{1,0:T(8,128)(2,1)S(1)}, bf16[256,1024]{1,0:T(8,128)(2,1)S(1)}, u32[]{:S(2)}, u32[]{:S(2)}) collective-permute-start(bf16[256,1024]{1,0:T(8,128)(2,1)S(1)} %pad_maximum_fusion), channel_id=1, source_target_pairs={{3,0},{4,1},{5,2},{6,3},{7,4},{8,5},{9,6},{10,7},{11,8},{12,9},{13... | collective-permute-start | bytes 1572872 | tf_op jit(solution)/shard_map/ppermute | solution.py:19
  153.8 48.8 %collective-permute-start.3 = (bf16[256,1024]{1,0:T(8,128)(2,1)S(1)}, bf16[256,1024]{1,0:T(8,128)(2,1)S(1)}, u32[]{:S(2)}, u32[]{:S(2)}) collective-permute-start(bf16[256,1024]{1,0:T(8,128)(2,1)S(1)} %pad_maximum_fusion), channel_id=1, source_target_pairs={{4,0},{5,1},{6,2},{7,3},{8,4},{9,5},{10,6},{11,7},{12,8},{13,9},{1... | collective-permute-start | bytes 1572872 | tf_op jit(solution)/shard_map/ppermute | solution.py:19
  155.1 49.8 %collective-permute-start.4 = (bf16[256,1024]{1,0:T(8,128)(2,1)S(1)}, bf16[256,1024]{1,0:T(8,128)(2,1)S(1)}, u32[]{:S(2)}, u32[]{:S(2)}) collective-permute-start(bf16[256,1024]{1,0:T(8,128)(2,1)S(1)} %pad_maximum_fusion), channel_id=1, source_target_pairs={{5,0},{6,1},{7,2},{8,3},{9,4},{10,5},{11,6},{12,7},{13,8},{14,9},{... | collective-permute-start | bytes 1572872 | tf_op jit(solution)/shard_map/ppermute | solution.py:19
  167.0 41.8 %collective-permute-start.5 = (bf16[256,1024]{1,0:T(8,128)(2,1)S(1)}, bf16[256,1024]{1,0:T(8,128)(2,1)S(1)}, u32[]{:S(2)}, u32[]{:S(2)}) collective-permute-start(bf16[256,1024]{1,0:T(8,128)(2,1)S(1)} %pad_maximum_fusion), channel_id=1, source_target_pairs={{6,0},{7,1},{8,2},{9,3},{10,4},{11,5},{12,6},{13,7},{14,8},{15,9},... | collective-permute-start | bytes 1572872 | tf_op jit(solution)/shard_map/ppermute | solution.py:19
  171.5 100.1 %collective-permute-start.6 = (bf16[256,1024]{1,0:T(8,128)(2,1)S(1)}, bf16[256,1024]{1,0:T(8,128)(2,1)S(1)}, u32[]{:S(2)}, u32[]{:S(2)}) collective-permute-start(bf16[256,1024]{1,0:T(8,128)(2,1)S(1)} %pad_maximum_fusion), channel_id=1, source_target_pairs={{7,0},{8,1},{9,2},{10,3},{11,4},{12,5},{13,6},{14,7},{15,8},{23,16... | collective-permute-start | bytes 1572872 | tf_op jit(solution)/shard_map/ppermute | solution.py:19
where the time goes:
time: 295 us; the launch traced here: 294 us
  waiting for transfers between devices  169 us (57%)
  matrix products  42.2 us (14%)
  local copies, waits for them, and re-layouts  40 us (14%)
  other arithmetic  24.9 us (8%)
  starting transfers between devices  17.3 us (6%)
    ppermute x7, waiting for transfers between devices, from_behind(): lax.ppermute(value, axis, [(source, source + steps) for source in range(i...  111 us
    all_to_all x1, waiting for transfers between devices, shards(): lax.all_to_all(raw, 'row', split_axis=0, concat_axis=1, tiled=True)  57.6 us
    dot_general x1, matrix products, whiten(): jnp.dot(decimated, spectral_table(), preferred_element_type=jnp.float32)  30.3 us
    transpose x2, local copies, waits for them, and re-layouts, fir_decimate(): phased = jnp.transpose(padded.reshape(rows, width // DEC, DEC), (2, 0, 1))  21.1 us
    another operation x2, other arithmetic  19.3 us
    convert_element_type x1, local copies, waits for them, and re-layouts, shards(): return (shaped * scales[None, None, :, None]).astype(jnp.bfloat16)  11.5 us
    dot_general x1, matrix products, shards(): lax.dot_general(lagged, column_block, (((1,), (1,)), ((), ())), preferred...  11.2 us
    ppermute x7, starting transfers between devices, from_behind(): lax.ppermute(value, axis, [(source, source + steps) for source in range(i...  9.83 us
  transfers between devices with their start and end apart: 8, of which 8 were waited for; matrix products, arithmetic and copies ran while one was open for 7% of the time, Pallas kernels for 0%

commit v1 on v0

--- a/solution.py
+++ b/solution.py
@@ -76,7 +76,9 @@
 def shards(raw, fir_taps, band_width, dead_count):
     band_span = band_width[0]
     dead_here = dead_count[0]
-    channel_block = lax.all_to_all(raw, "row", split_axis=0, concat_axis=1, tiled=True)
+    parts = jnp.split(raw, lax.axis_size("row"), axis=0)
+    incoming = lax.all_to_all(jnp.stack(parts), "row", 0, 0)
+    channel_block = jnp.concatenate(incoming, axis=1)
     padded = jnp.pad(channel_block.astype(jnp.float32), ((0, 0), (2 * DEC, 2 * DEC)))
     filtered = fir_decimate(padded, fir_taps, NT)
     tile_rows = filtered.shape[0]

time: 295 us -> 316 us (1.071)
  local copies, waits for them, and re-layouts: 40 us -> 59.9 us
    unnamed x8 -> x39, local copies, waits for them, and re-layouts: 0.22 us -> 22.6 us
    convert_element_type x1 -> x0, local copies, waits for them, and re-layouts: 6.38 us -> none  [shards(): channel_block.astype(jnp.float32)]
    split x0 -> x1, local copies, waits for them, and re-layouts: none -> 3.36 us  [shards(): parts = jnp.split(raw, lax.axis_size('row'), axis=0)]
where the time goes in v1:
time: 316 us; the launch traced here: 315 us
  waiting for transfers between devices  169 us (53%)
  local copies, waits for them, and re-layouts  59.9 us (19%)
  matrix products  42.3 us (13%)
  other arithmetic  24.9 us (8%)
  starting transfers between devices  17.3 us (5%)
    ppermute x7, waiting for transfers between devices, from_behind(): lax.ppermute(value, axis, [(source, source + steps) for source in range(i...  111 us
    all_to_all x1, waiting for transfers between devices, shards(): incoming = lax.all_to_all(jnp.stack(parts), 'row', 0, 0)  57.6 us
    dot_general x1, matrix products, whiten(): jnp.dot(decimated, spectral_table(), preferred_element_type=jnp.float32)  30.4 us
    unnamed x39, local copies, waits for them, and re-layouts  22.6 us
    transpose x2, local copies, waits for them, and re-layouts, fir_decimate(): phased = jnp.transpose(padded.reshape(rows, width // DEC, DEC), (2, 0, 1))  21 us
    another operation x2, other arithmetic  19.3 us
    convert_element_type x1, local copies, waits for them, and re-layouts, shards(): return (shaped * scales[None, None, :, None]).astype(jnp.bfloat16)  11.5 us
    dot_general x1, matrix products, shards(): lax.dot_general(lagged, column_block, (((1,), (1,)), ((), ())), preferred...  11.2 us
  transfers between devices with their start and end apart: 8, of which 8 were waited for; matrix products, arithmetic and copies ran while one was open for 7% of the time, Pallas kernels for 0%

profile of v1, /device:TPU:1, one launch (start us, length us, event | category | flops | bytes accessed | tf_op | source)
XLA Modules:
  0.0 314.6 jit_solution(7725385831266408182)
XLA Ops:
  0.0 3.4 %fusion.51 = (bf16[256,512]{1,0:T(8,128)(2,1)S(1)}, bf16[256,512]{1,0:T(8,128)(2,1)S(1)}, bf16[256,512]{1,0:T(8,128)(2,1)S(1)}, bf16[256,512]{1,0:T(8,128)(2,1)S...) fusion(bf16[4096,512]{1,0:T(8,128)(2,1)} %param.4), kind=kLoop, calls=%fused_computation.117 | loop fusion | bytes 8388608 | tf_op jit(solution)/shard_map/split | solution.py:79
  3.4 1.8 copy.59
  5.1 1.7 bitcast_dynamic-update-slice_fusion.22
  6.8 1.8 copy.60
  8.6 1.8 copy.61
  10.4 0.8 copy.62
  11.2 0.1 copy.63
  11.4 0.1 copy.64
  11.5 0.1 copy.65
  11.6 0.1 copy.66
  11.8 0.1 copy.67
  11.9 0.1 copy.68
  12.1 0.1 copy.69
  12.2 0.1 copy.70
  12.3 0.1 copy.71
  12.5 0.1 copy.72
  12.6 0.1 copy.73
  12.8 0.1 copy.74
  12.9 1.7 bitcast_dynamic-update-slice_fusion.21
  14.6 1.7 bitcast_dynamic-update-slice_fusion.20
  16.2 1.7 bitcast_dynamic-update-slice_fusion.19
  17.9 0.7 bitcast_dynamic-update-slice_fusion.18
  18.6 0.7 bitcast_dynamic-update-slice_fusion.17
  19.4 0.7 bitcast_dynamic-update-slice_fusion.16
  20.1 0.7 bitcast_dynamic-update-slice_fusion.15
  20.8 0.7 bitcast_dynamic-update-slice_fusion.14
  21.5 0.7 bitcast_dynamic-update-slice_fusion.13
  22.2 0.7 bitcast_dynamic-update-slice_fusion.12
  23.0 0.7 bitcast_dynamic-update-slice_fusion.11
  23.7 0.7 bitcast_dynamic-update-slice_fusion.10
  24.4 0.7 bitcast_dynamic-update-slice_fusion.9
  25.1 0.7 bitcast_dynamic-update-slice_fusion.8
  25.8 0.7 bitcast_dynamic-update-slice_fusion.7
  26.6 7.5 %all-to-all-start = ((bf16[16,256,512]{1,2,0:T(8,128)(2,1)}), bf16[16,256,512]{1,2,0:T(8,128)(2,1)}, u32[]{:S(2)}, u32[]{:S(2)}) async-start(bf16[16,256,512]{1,2,0:T(8,128)(2,1)} %bitcast_dynamic-update-slice_fusion.7), calls=%async_computation | async-start | bytes 8388608 | tf_op jit(solution)/shard_map/all_to_all | solution.py:80
  35.3 0.1 convert_reduce_fusion
  35.5 0.0 copy-done
  35.5 0.7 fusion.52
  36.2 0.2 fusion.44
  36.3 18.2 %cosine_convert_fusion = (bf16[2048,512]{1,0:T(8,128)(2,1)S(1)}, bf16[2048,512]{1,0:T(8,128)(2,1)}) fusion(s32[512]{0:T(512)S(1)} %iota_add_fusion), kind=kLoop, calls=%fused_computation.19 | loop fusion | flops 17825792 | bytes 4196352 | tf_op jit(solution)/shard_map/convert.14
  54.5 57.6 %all-to-all-done = bf16[16,256,512]{1,2,0:T(8,128)(2,1)} async-done(((bf16[16,256,512]{1,2,0:T(8,128)(2,1)}), bf16[16,256,512]{1,2,0:T(8,128)(2,1)}, u32[]{:S(2)}, u32[]{:S(2)}) %all-to-all-start) | async-done | bytes 4194336 | tf_op jit(solution)/shard_map/all_to_all | solution.py:80
  112.1 5.1 %pad_convert_fusion = f32[256,8208]{0,1:T(8,128)} fusion(bf16[256,8192]{0,1:T(8,128)(2,1)} %bitcast.18), kind=kLoop, calls=%fused_computation.4 | loop fusion | flops 2101248 | bytes 12599296 | tf_op jit(solution)/shard_map/transpose | solution.py:26
  117.3 10.1 %reshape.191 = f32[256,2052,4]{0,2,1:T(4,128)} reshape(f32[256,8208]{0,1:T(8,128)} %pad_convert_fusion) | data formatting | bytes 16809984 | tf_op jit(solution)/shard_map/transpose | solution.py:26
  127.4 10.8 %copy.56 = f32[256,2052,4]{1,0,2:T(8,128)} copy(f32[256,2052,4]{0,2,1:T(4,128)} %reshape.191) | data formatting | bytes 16809984 | tf_op jit(solution)/shard_map/transpose | solution.py:26
  138.2 30.4 %fusion.3 = f32[256,1024]{1,0:T(8,128)S(1)} fusion(bf16[2048,512]{1,0:T(8,128)(2,1)} %get-tuple-element.32, bf16[2048,512]{1,0:T(8,128)(2,1)S(1)} %get-tuple-element.31, f32[4,256,2052]{2,1,0:T(8,128)} %bitcast.89, f32[256]{0:T(256)S(1)} %compare_convert_fusion, f32[]{:T(128)} %bitcast.34, f32[]{:T(128)} %bitcast.33, f32[]{:T(128)} %bitcast.32, ...), kind=kOutput, calls=%fused_computation.8 | convolution fusion | flops 1099431936 | bytes 38806528 | tf_op jit(solution)/shard_map/dot_general | solution.py:45
  168.6 0.7 fusion.49
  169.4 0.1 pad_maximum_fusion
  169.4 1.9 collective-permute-start
  171.4 1.3 collective-permute-start.1
  172.7 1.3 collective-permute-start.2
  174.0 1.3 collective-permute-start.3
  175.3 1.5 collective-permute-start.4
  176.7 1.1 subtract_convert_fusion
  177.9 0.1 maximum_dynamic-update-slice_fusion
  177.9 9.3 %collective-permute-done = bf16[256,1024]{1,0:T(8,128)(2,1)S(1)} collective-permute-done((bf16[256,1024]{1,0:T(8,128)(2,1)S(1)}, bf16[256,1024]{1,0:T(8,128)(2,1)S(1)}, u32[]{:S(2)}, u32[]{:S(2)}) %collective-permute-start) | collective-permute-done | bytes 524320 | tf_op jit(solution)/shard_map/ppermute | solution.py:19
  187.3 1.3 collective-permute-start.5
  188.6 3.1 collective-permute-done.1
  191.7 1.3 collective-permute-start.6
  193.1 25.8 %collective-permute-done.2 = bf16[256,1024]{1,0:T(8,128)(2,1)S(1)} collective-permute-done((bf16[256,1024]{1,0:T(8,128)(2,1)S(1)}, bf16[256,1024]{1,0:T(8,128)(2,1)S(1)}, u32[]{:S(2)}, u32[]{:S(2)}) %collective-permute-start.2) | collective-permute-done | bytes 524320 | tf_op jit(solution)/shard_map/ppermute | solution.py:19
  218.9 3.9 %collective-permute-done.3 = bf16[256,1024]{1,0:T(8,128)(2,1)S(1)} collective-permute-done((bf16[256,1024]{1,0:T(8,128)(2,1)S(1)}, bf16[256,1024]{1,0:T(8,128)(2,1)S(1)}, u32[]{:S(2)}, u32[]{:S(2)}) %collective-permute-start.3) | collective-permute-done | bytes 524320 | tf_op jit(solution)/shard_map/ppermute | solution.py:19
  222.8 2.3 collective-permute-done.4
  225.2 3.9 %collective-permute-done.5 = bf16[256,1024]{1,0:T(8,128)(2,1)S(1)} collective-permute-done((bf16[256,1024]{1,0:T(8,128)(2,1)S(1)}, bf16[256,1024]{1,0:T(8,128)(2,1)S(1)}, u32[]{:S(2)}, u32[]{:S(2)}) %collective-permute-start.5) | collective-permute-done | bytes 524320 | tf_op jit(solution)/shard_map/ppermute | solution.py:19
  229.1 62.7 %collective-permute-done.6 = bf16[256,1024]{1,0:T(8,128)(2,1)S(1)} collective-permute-done((bf16[256,1024]{1,0:T(8,128)(2,1)S(1)}, bf16[256,1024]{1,0:T(8,128)(2,1)S(1)}, u32[]{:S(2)}, u32[]{:S(2)}) %collective-permute-start.6) | collective-permute-done | bytes 524320 | tf_op jit(solution)/shard_map/ppermute | solution.py:19
  291.8 11.2 %multiply_convert_fusion = bf16[256,8,8,256]{3,0,2,1:T(8,128)(2,1)} fusion(f32[8]{0:T(128)S(1)} %compare_select_fusion.2, bf16[256,8,512]{2,0,1:T(8,128)(2,1)S(1)} %get-tuple-element.28, bf16[256,8,512]{2,0,1:T(8,128)(2,1)S(1)} %get-tuple-element.27, bf16[8,256,1024]{2,1,0:T(8,128)(2,1)S(1)} %bitcast_dynamic-update-slice_fusion), kind=kOutput, calls=%fused_computation | convolution fusion | flops 8606711808 | bytes 16777248 | tf_op jit(solution)/shard_map/dot_general | solution.py:96
  303.0 11.5 %copy.57 = bf16[256,8,8,256]{3,2,1,0:T(8,128)(2,1)} copy(bf16[256,8,8,256]{3,0,2,1:T(8,128)(2,1)} %multiply_convert_fusion) | data formatting | bytes 16777216 | tf_op jit(solution)/shard_map/convert_element_type | solution.py:100
  (12 shorter events, 0.3 us)
Async XLA Ops:
  26.6 8.9 %copy-start = (f32[16]{0:T(128)S(1)}, f32[16]{0:T(128)}, u32[]{:S(2)}) copy-start(f32[16]{0:T(128)} %param.5) | copy-start | bytes 196
  26.6 85.5 %all-to-all-start = ((bf16[16,256,512]{1,2,0:T(8,128)(2,1)}), bf16[16,256,512]{1,2,0:T(8,128)(2,1)}, u32[]{:S(2)}, u32[]{:S(2)}) async-start(bf16[16,256,512]{1,2,0:T(8,128)(2,1)} %bitcast_dynamic-update-slice_fusion.7), calls=%async_computation | async-start | bytes 8388608 | tf_op jit(solution)/shard_map/all_to_all | solution.py:80
  169.4 17.8 %collective-permute-start = (bf16[256,1024]{1,0:T(8,128)(2,1)S(1)}, bf16[256,1024]{1,0:T(8,128)(2,1)S(1)}, u32[]{:S(2)}, u32[]{:S(2)}) collective-permute-start(bf16[256,1024]{1,0:T(8,128)(2,1)S(1)} %pad_maximum_fusion), channel_id=1, source_target_pairs={{1,0},{2,1},{3,2},{4,3},{5,4},{6,5},{7,6},{8,7},{9,8},{10,9},{11,1... | collective-permute-start | bytes 1572872 | tf_op jit(solution)/shard_map/ppermute | solution.py:19
  171.4 20.4 %collective-permute-start.1 = (bf16[256,1024]{1,0:T(8,128)(2,1)S(1)}, bf16[256,1024]{1,0:T(8,128)(2,1)S(1)}, u32[]{:S(2)}, u32[]{:S(2)}) collective-permute-start(bf16[256,1024]{1,0:T(8,128)(2,1)S(1)} %pad_maximum_fusion), channel_id=1, source_target_pairs={{2,0},{3,1},{4,2},{5,3},{6,4},{7,5},{8,6},{9,7},{10,8},{11,9},{12,... | collective-permute-start | bytes 1572872 | tf_op jit(solution)/shard_map/ppermute | solution.py:19
  172.7 46.2 %collective-permute-start.2 = (bf16[256,1024]{1,0:T(8,128)(2,1)S(1)}, bf16[256,1024]{1,0:T(8,128)(2,1)S(1)}, u32[]{:S(2)}, u32[]{:S(2)}) collective-permute-start(bf16[256,1024]{1,0:T(8,128)(2,1)S(1)} %pad_maximum_fusion), channel_id=1, source_target_pairs={{3,0},{4,1},{5,2},{6,3},{7,4},{8,5},{9,6},{10,7},{11,8},{12,9},{13... | collective-permute-start | bytes 1572872 | tf_op jit(solution)/shard_map/ppermute | solution.py:19
  174.0 48.8 %collective-permute-start.3 = (bf16[256,1024]{1,0:T(8,128)(2,1)S(1)}, bf16[256,1024]{1,0:T(8,128)(2,1)S(1)}, u32[]{:S(2)}, u32[]{:S(2)}) collective-permute-start(bf16[256,1024]{1,0:T(8,128)(2,1)S(1)} %pad_maximum_fusion), channel_id=1, source_target_pairs={{4,0},{5,1},{6,2},{7,3},{8,4},{9,5},{10,6},{11,7},{12,8},{13,9},{1... | collective-permute-start | bytes 1572872 | tf_op jit(solution)/shard_map/ppermute | solution.py:19
  175.3 49.9 %collective-permute-start.4 = (bf16[256,1024]{1,0:T(8,128)(2,1)S(1)}, bf16[256,1024]{1,0:T(8,128)(2,1)S(1)}, u32[]{:S(2)}, u32[]{:S(2)}) collective-permute-start(bf16[256,1024]{1,0:T(8,128)(2,1)S(1)} %pad_maximum_fusion), channel_id=1, source_target_pairs={{5,0},{6,1},{7,2},{8,3},{9,4},{10,5},{11,6},{12,7},{13,8},{14,9},{... | collective-permute-start | bytes 1572872 | tf_op jit(solution)/shard_map/ppermute | solution.py:19
  187.3 41.8 %collective-permute-start.5 = (bf16[256,1024]{1,0:T(8,128)(2,1)S(1)}, bf16[256,1024]{1,0:T(8,128)(2,1)S(1)}, u32[]{:S(2)}, u32[]{:S(2)}) collective-permute-start(bf16[256,1024]{1,0:T(8,128)(2,1)S(1)} %pad_maximum_fusion), channel_id=1, source_target_pairs={{6,0},{7,1},{8,2},{9,3},{10,4},{11,5},{12,6},{13,7},{14,8},{15,9},... | collective-permute-start | bytes 1572872 | tf_op jit(solution)/shard_map/ppermute | solution.py:19
  191.7 100.1 %collective-permute-start.6 = (bf16[256,1024]{1,0:T(8,128)(2,1)S(1)}, bf16[256,1024]{1,0:T(8,128)(2,1)S(1)}, u32[]{:S(2)}, u32[]{:S(2)}) collective-permute-start(bf16[256,1024]{1,0:T(8,128)(2,1)S(1)} %pad_maximum_fusion), channel_id=1, source_target_pairs={{7,0},{8,1},{9,2},{10,3},{11,4},{12,5},{13,6},{14,7},{15,8},{23,16... | collective-permute-start | bytes 1572872 | tf_op jit(solution)/shard_map/ppermute | solution.py:19
